TPU v7x, 128 devices: a whole 4x4x4 slice. The times are simulated.
128 devices in a mesh: owner: 4 (over y), worker: 32 (over x, z, core).
Axes of the slice: x: 4, y: 4, z: 4, core: 2. Of those that a mesh axis runs over, the one named last changes fastest.
Arguments:
- states: float32 [262144, 512], P(('owner', 'worker')), may hold values from -3 to 3
- row_of_user: int32 [262144], replicated, may hold values from 0 to 262143, as said below
- event_users: int32 [65536], P(('owner', 'worker')), may hold values from 0 to 262143, as said below
- event_features: int32 [65536], P(('owner', 'worker')), may hold values from 0 to 4095
- feature_table: bfloat16 [4096, 512], replicated, may hold values from -6 to 6
- gate_in: bfloat16 [512, 1536], replicated, may hold values from -0.25 to 0.25
- gate_state: bfloat16 [512, 1536], replicated, may hold values from -0.25 to 0.25
- tower_in: bfloat16 [4096, 1024], P(('owner', 'worker')), may hold values from -0.1875 to 0.1875
- tower_out: bfloat16 [512, 4096], P(('owner', 'worker')), may hold values from -0.09375 to 0.09375
Outputs:
- new_states: float32 [262144, 512], P(('owner', 'worker'))
- scores: float32 [65536], P(('owner', 'worker'))
Inputs may be any that keep to these rules, and one draw needn't show every extreme that they name: `row_of_user`: A permutation: each user has its own state row. `event_users`: among the 512 events of one device, at most 8 have their row (row_of_user of the user) in one device's block of 2048 rows, and for every device some block receives exactly 8 of its events.
All inputs are finite; a program needn't handle non-finite values.
Results may differ from a plain program's by a relative error of at most 0.0034.
Values may be sent and summed in bfloat16 or wider, within the bound.
A program may use at most 128 MiB of HBM per device.

v0:
```python
import jax
import jax.numpy as jnp
from jax import lax
from jax.sharding import PartitionSpec as P

AXES = ("owner", "worker")


def gru_cell(inputs, prior, gate_in, gate_state):
    gx = jnp.dot(inputs, gate_in, preferred_element_type=jnp.float32)
    gh = jnp.dot(prior, gate_state, preferred_element_type=jnp.float32)
    width = prior.shape[-1]
    reset = jax.nn.sigmoid(gx[:, :width] + gh[:, :width])
    update = jax.nn.sigmoid(gx[:, width : 2 * width] + gh[:, width : 2 * width])
    cand = jnp.tanh(gx[:, 2 * width :] + reset * gh[:, 2 * width :])
    return (1.0 - update) * cand + update * prior.astype(jnp.float32)


def per_device(
    states,
    row_of_user,
    event_users,
    event_features,
    feature_table,
    gate_in,
    gate_state,
    tower_in,
    tower_out,
):
    shards = lax.axis_size(AXES)
    events = event_users.shape[0]
    row_count, width = states.shape
    cap = 2 * (events // shards)
    rows = row_of_user[event_users]
    target = rows // row_count
    local = rows - target * row_count
    hits = (target[:, None] == jnp.arange(shards, dtype=jnp.int32)[None, :]).astype(jnp.int32)
    rank = jnp.sum((jnp.cumsum(hits, axis=0) - hits) * hits, axis=1)
    slot = target * cap + rank
    packed = local + row_count * event_features
    requests = jnp.full((shards * cap,), -1, jnp.int32).at[slot].set(packed).reshape(shards, cap)
    asked = lax.all_to_all(requests, AXES, split_axis=0, concat_axis=0, tiled=True).reshape(-1)
    valid = asked >= 0
    owned = jnp.where(valid, asked, 0)
    owned_feature = owned // row_count
    owned_row = owned - owned_feature * row_count
    prior = states[owned_row].astype(jnp.bfloat16)
    inputs = feature_table[owned_feature]
    fresh = gru_cell(inputs, prior, gate_in, gate_state)
    delta = fresh - prior.astype(jnp.float32)
    ids = jnp.where(valid, owned_row, row_count)
    total = jax.ops.segment_sum(delta, ids, num_segments=row_count + 1)[:row_count]
    count = jax.ops.segment_sum(valid.astype(jnp.int32), ids, num_segments=row_count + 1)[
        :row_count
    ]
    new_states = states + total / jnp.maximum(count, 1).astype(jnp.float32)[:, None]
    joined = jnp.concatenate([fresh.astype(jnp.bfloat16), inputs], axis=1)
    hidden = jax.nn.gelu(
        lax.dot_general(
            joined,
            lax.all_gather(tower_in, AXES, axis=0, tiled=True),
            (((1,), (1,)), ((), ())),
            preferred_element_type=jnp.float32,
        )
    ).astype(jnp.bfloat16)
    tower = lax.dot_general(
        hidden,
        lax.all_gather(tower_out, AXES, axis=0, tiled=True),
        (((1,), (1,)), ((), ())),
        preferred_element_type=jnp.float32,
    )
    scored = jnp.sum(tower * inputs.astype(jnp.float32), axis=1) / jnp.sqrt(jnp.float32(width))
    back = lax.all_to_all(
        scored.reshape(shards, cap), AXES, split_axis=0, concat_axis=0, tiled=True
    )
    return (new_states, back.reshape(-1)[slot])


def solution(mesh):
    placed = (P(AXES, None), P(), P(AXES), P(AXES), P(), P(), P(), P(AXES, None), P(AXES, None))
    return jax.shard_map(
        per_device, mesh=mesh, in_specs=placed, out_specs=(P(AXES, None), P(AXES)), check_vma=False
    )
```

profile of v0, /device:TPU:1, one launch (start us, length us, event | category | flops | bytes accessed | tf_op | source)
XLA Modules:
  0.0 198.0 jit_solution(6553455652774412179)
XLA Ops:
  7.2 0.7 all-gather.6.cloned.1.call-update
  8.0 0.7 all-gather.4.cloned.1.call-update
  8.7 0.7 compare_select_fusion.8
  9.4 6.5 %gather_fusion = s32[512]{0:T(512)S(1)} fusion(s32[262144]{0:T(1024)} %param.10, s32[1024]{0:T(1024)S(1)} %pad_clamp_fusion.1), kind=kCustom, calls=%fused_computation | custom fusion | bytes 6144 | tf_op jit(solution)/shard_map/gather | solution.py:34
  15.9 0.1 copy.15
  16.0 0.2 fusion.41
  16.4 0.2 fusion.40
  16.6 2.4 %scatter_custom_fusion = s32[1024]{0:T(1024)S(1)} fusion(s32[512]{0:T(512)S(1)} %bitcast.51, s32[512]{0:T(512)S(1)} %get-tuple-element.10, s32[]{:T(128)} %constant.20.clone.1), kind=kCustom, calls=%fused_computation.94 | custom fusion | bytes 4100 | tf_op jit(solution)/shard_map/scatter | solution.py:41
  19.1 0.7 all_to_all.10
  19.8 11.5 %all-to-all-start = ((s32[128,1,8]{2,1,0:T(1,128)}), s32[128,1,8]{2,1,0:T(1,128)S(1)}, u32[]{:S(2)}, u32[]{:S(2)}) async-start(s32[128,1,8]{2,1,0:T(1,128)} %bitcast.7), calls=%async_computation | async-start | bytes 131072 | tf_op jit(solution)/shard_map/all_to_all | solution.py:42
  31.3 9.3 %all-to-all-done = s32[128,1,8]{2,1,0:T(1,128)S(1)} async-done(((s32[128,1,8]{2,1,0:T(1,128)}), s32[128,1,8]{2,1,0:T(1,128)S(1)}, u32[]{:S(2)}, u32[]{:S(2)}) %all-to-all-start) | async-done | bytes 4128 | tf_op jit(solution)/shard_map/all_to_all | solution.py:42
  40.6 0.5 broadcast.392
  41.1 1.0 fusion.44
  42.4 6.7 %gather_fusion.1 = bf16[1024,512]{1,0:T(8,128)(2,1)S(1)} fusion(bf16[4096,512]{1,0:T(8,128)(2,1)} %param.13, s32[1024]{0:T(1024)S(1)} %broadcast_clamp_fusion.1), kind=kCustom, calls=%fused_computation.1 | custom fusion | bytes 2101248 | tf_op jit(solution)/shard_map/gather | solution.py:48
  49.1 1.3 copy.18
  50.5 7.5 %gather_fusion.2 = f32[1024,512]{1,0:T(8,128)} fusion(f32[2048,512]{1,0:T(8,128)} %param.9, s32[1024]{0:T(1024)S(1)} %broadcast_clamp_fusion), kind=kCustom, calls=%fused_computation.2 | custom fusion | bytes 4198400 | tf_op jit(solution)/shard_map/gather | solution.py:47
  57.9 6.9 %scatter_custom_fusion.2 = s32[2049]{0:T(1024)S(1)} fusion(s32[1024]{0:T(1024)S(1)} %bitcast.53, s32[1024]{0:T(1024)S(1)} %reshape.288, s32[]{:T(128)} %constant.21.clone.1), kind=kCustom, calls=%fused_computation.66 | custom fusion | flops 1024 | bytes 8200 | tf_op jit(solution)/shard_map/scatter-add | solution.py:53
  64.9 1.8 fusion.66
  66.7 0.2 copy-done.2
  66.9 1.8 fusion.61
  68.7 3.1 %fusion.64 = (bf16[1024,512]{1,0:T(8,128)(2,1)}, f32[1024,512]{1,0:T(8,128)}) fusion(f32[1024,512]{1,0:T(8,128)S(1)} %copy-done.1, f32[1024,1536]{1,0:T(8,128)S(1)} %fusion.61, f32[1024,1536]{1,0:T(8,128)S(1)} %fusion.66), kind=kLoop, calls=%fused_computation.106 | loop fusion | flops 8912896 | bytes 17825792 | tf_op jit(solution)/shard_map/convert_element_type | solution.py:57
  71.8 10.3 %scatter_custom_fusion.1 = f32[2049,512]{1,0:T(8,128)} fusion(s32[1024]{0:T(1024)S(1)} %bitcast.54, f32[]{:T(128)} %constant.19.clone.1, f32[1024,512]{1,0:T(8,128)} %get-tuple-element.5, f32[1024,512]{1,0:T(8,128)} %gather_fusion.2), kind=kCustom, calls=%fused_computation.21 | custom fusion | flops 2097152 | bytes 8390660 | tf_op jit(solution)/shard_map/scatter-add | solution.py:52
  82.1 6.9 %reshape.294 = bf16[512,4096]{1,0:T(8,128)(2,1)} reshape(bf16[128,4,4096]{2,1,0:T(4,128)(2,1)} %all-gather.6.cloned.1.call-done) | data formatting | bytes 8388608
  89.0 63.4 %all-gather.4.cloned.1.call-done = bf16[4096,1024]{1,0:T(8,128)(2,1)} async-done(((bf16[32,1024]{1,0:T(8,128)(2,1)}), bf16[4096,1024]{1,0:T(8,128)(2,1)}) %all-gather.4.cloned.1.call-update) | async-done | bytes 8388624 | tf_op jit(solution)/shard_map/all_gather | solution.py:61
  152.4 18.4 %multiply_reduce_fusion = f32[1024]{0:T(1024)S(1)} fusion(bf16[1024,512]{0,1:T(8,128)(2,1)} %copy.18, bf16[512,4096]{1,0:T(8,128)(2,1)} %reshape.294, bf16[4096,1024]{1,0:T(8,128)(2,1)} %all-gather.4.cloned.1.call-done, bf16[1024,512]{1,0:T(8,128)(2,1)S(1)} %gather_fusion.1, bf16[1024,512]{1,0:T(8,128)(2,1)} %get-tuple-element.4), kind=kOutput, calls=%fused_computation.42 | convolution fusion | flops 12928416768 | bytes 15732736 | tf_op jit(solution)/shard_map/dot_general | solution.py:66
  170.8 0.7 div.84
  171.5 5.4 %all-to-all-start.1 = ((f32[128,1,8]{2,1,0:T(1,128)}), f32[128,1,8]{2,1,0:T(1,128)S(1)}, u32[]{:S(2)}, u32[]{:S(2)}) async-start(f32[128,1,8]{2,1,0:T(1,128)} %bitcast.12), calls=%async_computation.1 | async-start | bytes 131072 | tf_op jit(solution)/shard_map/all_to_all | solution.py:73
  176.9 6.0 %fusion.10 = f32[2048,512]{1,0:T(8,128)} fusion(f32[2048,512]{1,0:T(8,128)} %param.9, f32[2049,512]{1,0:T(8,128)} %scatter_custom_fusion.1, f32[2048]{0:T(1024)S(1)} %fusion.45), kind=kLoop, calls=%fused_computation.18 | loop fusion | flops 2097152 | bytes 12591104 | tf_op jit(solution)/shard_map/add | solution.py:56
  182.9 3.4 %all-to-all-done.1 = f32[128,1,8]{2,1,0:T(1,128)S(1)} async-done(((f32[128,1,8]{2,1,0:T(1,128)}), f32[128,1,8]{2,1,0:T(1,128)S(1)}, u32[]{:S(2)}, u32[]{:S(2)}) %all-to-all-start.1) | async-done | bytes 4128 | tf_op jit(solution)/shard_map/all_to_all | solution.py:73
  186.3 0.5 broadcast.393
  186.8 0.8 reduce.11
  187.7 3.4 %gather_fusion.3 = f32[512]{0:T(512)} fusion(f32[1024]{0:T(1024)S(1)} %reshape.234, s32[1024]{0:T(1024)S(1)} %pad_clamp_fusion), kind=kCustom, calls=%fused_computation.3 | custom fusion | bytes 6144 | tf_op jit(solution)/shard_map/gather | solution.py:76
  (30 shorter events, 0.6 us)
Async XLA Ops:
  7.2 57.7 %copy-start = (bf16[512,1536]{1,0:T(8,128)(2,1)S(1)}, bf16[512,1536]{1,0:T(8,128)(2,1)}, u32[]{:S(2)}) copy-start(bf16[512,1536]{1,0:T(8,128)(2,1)} %param.14) | copy-start | bytes 4718596
  7.2 9.1 %copy-start.3 = (s32[512]{0:T(512)S(1)}, s32[512]{0:T(512)}, u32[]{:S(2)}) copy-start(s32[512]{0:T(512)} %param.12) | copy-start | bytes 6148
  7.2 74.9 %all-gather.6.cloned.1.call-start = ((), (), s32[]{:S(2)}) async-start(), calls=%async_computation.3 | async-start | bytes 4227072 | tf_op jit(solution)/shard_map/all_gather | solution.py:68
  7.9 144.4 %all-gather.4.cloned.1.call-start = ((), (), s32[]{:S(2)}) async-start(), calls=%async_computation.2 | async-start | bytes 8454144 | tf_op jit(solution)/shard_map/all_gather | solution.py:61
  19.8 20.8 %all-to-all-start = ((s32[128,1,8]{2,1,0:T(1,128)}), s32[128,1,8]{2,1,0:T(1,128)S(1)}, u32[]{:S(2)}, u32[]{:S(2)}) async-start(s32[128,1,8]{2,1,0:T(1,128)} %bitcast.7), calls=%async_computation | async-start | bytes 131072 | tf_op jit(solution)/shard_map/all_to_all | solution.py:42
  64.9 1.8 copy-start.1
  64.9 2.0 %copy-start.2 = (bf16[512,1536]{1,0:T(8,128)(2,1)S(1)}, bf16[512,1536]{1,0:T(8,128)(2,1)}, u32[]{:S(2)}) copy-start(bf16[512,1536]{1,0:T(8,128)(2,1)} %param.15) | copy-start | bytes 4718596
  171.5 14.8 %all-to-all-start.1 = ((f32[128,1,8]{2,1,0:T(1,128)}), f32[128,1,8]{2,1,0:T(1,128)S(1)}, u32[]{:S(2)}, u32[]{:S(2)}) async-start(f32[128,1,8]{2,1,0:T(1,128)} %bitcast.12), calls=%async_computation.1 | async-start | bytes 131072 | tf_op jit(solution)/shard_map/all_to_all | solution.py:73
Sparse Core Ops, SparseCore 0:
  11.2 70.5 all-gather.5
  84.8 67.5 all-gather.3
where the time goes:
time: 199 us; the launch traced here: 198 us
  waiting for transfers between devices  77.5 us (39%)
  local copies, waits for them, and re-layouts  37.9 us (19%)
  other arithmetic  29.4 us (15%)
  matrix products  22 us (11%)
  starting transfers between devices  17 us (9%)
  between operations  14.3 us (7%)
    all_gather x1, waiting for transfers between devices, per_device(): lax.all_gather(tower_in, AXES, axis=0, tiled=True)  63.4 us
    dot_general x1, matrix products, per_device(): lax.dot_general(hidden, lax.all_gather(tower_out, AXES, axis=0, tiled=Tru...  18.4 us
    all_to_all x1, starting transfers between devices, per_device(): lax.all_to_all(requests, AXES, split_axis=0, concat_axis=0, tiled=True)  11.5 us
    scatter-add x1, other arithmetic, per_device(): jax.ops.segment_sum(delta, ids, num_segments=row_count + 1)[:row_count]  10.3 us
    all_to_all x1, waiting for transfers between devices, per_device(): lax.all_to_all(requests, AXES, split_axis=0, concat_axis=0, tiled=True)  9.32 us
    gather x2, local copies, waits for them, and re-layouts, per_device(): inputs = feature_table[owned_feature]  8.05 us
    gather x1, local copies, waits for them, and re-layouts, per_device(): prior = states[owned_row].astype(jnp.bfloat16)  7.46 us
    unnamed x10, local copies, waits for them, and re-layouts  7.12 us
  transfers between devices with their start and end apart: 4, of which 3 were waited for; matrix products, arithmetic and copies ran while one was open for 32% of the time, Pallas kernels for 0%

commit v1 on v0

--- a/solution.py
+++ b/solution.py
@@ -4,6 +4,15 @@
 from jax.sharding import PartitionSpec as P
 
 AXES = ("owner", "worker")
+
+
+def _try_all_circles(arr, comm_axis):
+    mat_out = tuple((arr for _ in range(jax.lax.axis_size(comm_axis))))
+    response = jax.lax.all_to_all(
+        jnp.stack(mat_out), axis_name=comm_axis, split_axis=0, concat_axis=0
+    )
+    step_out = jnp.concatenate(response, axis=0)
+    return step_out
 
 
 def gru_cell(inputs, prior, gate_in, gate_state):
@@ -58,7 +67,7 @@
     hidden = jax.nn.gelu(
         lax.dot_general(
             joined,
-            lax.all_gather(tower_in, AXES, axis=0, tiled=True),
+            _try_all_circles(tower_in, AXES),
             (((1,), (1,)), ((), ())),
             preferred_element_type=jnp.float32,
         )

time: 199 us -> 238 us (1.20)
  waiting for transfers between devices: 77.5 us -> 107 us
  starting transfers between devices: 17 us -> 22.7 us
  local copies, waits for them, and re-layouts: 37.9 us -> 42.2 us
    all_gather x1, waiting for transfers between devices: 0.01 us -> 94.2 us  [per_device(): lax.all_gather(tower_out, AXES, axis=0, tiled=True)]
    all_gather x1 -> x0, waiting for transfers between devices: 63.4 us -> none  [per_device(): lax.all_gather(tower_in, AXES, axis=0, tiled=True)]
    all_to_all x0 -> x1, starting transfers between devices: none -> 5.82 us  [_try_all_circles(): jax.lax.all_to_all(jnp.stack(mat_out), axis_name=comm_axis, split_axis=0,...]
    another operation x3 -> x4, local copies, waits for them, and re-layouts: 0.03 us -> 4.31 us  [the longest x1 4.28 us: _try_all_circles(): jnp.stack(mat_out)]
    unnamed x10 -> x14, local copies, waits for them, and re-layouts: 7.12 us -> 7.13 us
  transfers between devices with their start and end apart: 4 -> 4, of which waited for: 3 -> 3; matrix products, arithmetic and copies ran while one was open for 32% -> 24% of each run, Pallas kernels for 0% -> 0%
where the time goes in v1:
time: 238 us; the launch traced here: 237 us
  waiting for transfers between devices  107 us (45%)
  local copies, waits for them, and re-layouts  42.2 us (18%)
  other arithmetic  29.2 us (12%)
  starting transfers between devices  22.7 us (10%)
  matrix products  21.8 us (9%)
  between operations  14.3 us (6%)
    all_gather x1, waiting for transfers between devices, per_device(): lax.all_gather(tower_out, AXES, axis=0, tiled=True)  94.2 us
    dot_general x1, matrix products, per_device(): lax.dot_general(hidden, lax.all_gather(tower_out, AXES, axis=0, tiled=Tru...  18.2 us
    all_to_all x1, starting transfers between devices, per_device(): lax.all_to_all(requests, AXES, split_axis=0, concat_axis=0, tiled=True)  11.5 us
    scatter-add x1, other arithmetic, per_device(): jax.ops.segment_sum(delta, ids, num_segments=row_count + 1)[:row_count]  10.2 us
    all_to_all x1, waiting for transfers between devices, per_device(): lax.all_to_all(requests, AXES, split_axis=0, concat_axis=0, tiled=True)  8.59 us
    gather x2, local copies, waits for them, and re-layouts, per_device(): inputs = feature_table[owned_feature]  8.05 us
    gather x1, local copies, waits for them, and re-layouts, per_device(): prior = states[owned_row].astype(jnp.bfloat16)  7.46 us
    unnamed x14, local copies, waits for them, and re-layouts  7.13 us
  transfers between devices with their start and end apart: 4, of which 3 were waited for; matrix products, arithmetic and copies ran while one was open for 24% of the time, Pallas kernels for 0%

profile of v1, /device:TPU:1, one launch (start us, length us, event | category | flops | bytes accessed | tf_op | source)
XLA Modules:
  0.0 237.0 jit_solution(8702147537769729699)
XLA Ops:
  7.2 0.8 compare_select_fusion.8
  8.0 6.5 %gather_fusion = s32[512]{0:T(512)S(1)} fusion(s32[262144]{0:T(1024)} %param.10, s32[1024]{0:T(1024)S(1)} %pad_clamp_fusion.1), kind=kCustom, calls=%fused_computation | custom fusion | bytes 6144 | tf_op jit(solution)/shard_map/gather | solution.py:43
  14.7 0.2 fusion.41
  15.0 0.2 fusion.40
  15.3 2.4 %scatter_custom_fusion = s32[1024]{0:T(1024)S(1)} fusion(s32[512]{0:T(512)S(1)} %bitcast.52, s32[512]{0:T(512)S(1)} %get-tuple-element.10, s32[]{:T(128)} %constant.20.clone.1), kind=kCustom, calls=%fused_computation.94 | custom fusion | bytes 4100 | tf_op jit(solution)/shard_map/scatter | solution.py:50
  17.7 0.7 all_to_all.13
  18.4 11.5 %all-to-all-start = ((s32[128,1,8]{2,1,0:T(1,128)}), s32[128,1,8]{2,1,0:T(1,128)S(1)}, u32[]{:S(2)}, u32[]{:S(2)}) async-start(s32[128,1,8]{2,1,0:T(1,128)} %bitcast.7), calls=%async_computation | async-start | bytes 131072 | tf_op jit(solution)/shard_map/all_to_all | solution.py:51
  30.0 0.7 all-gather.3.cloned.1.call-update
  30.7 8.6 %all-to-all-done = s32[128,1,8]{2,1,0:T(1,128)S(1)} async-done(((s32[128,1,8]{2,1,0:T(1,128)}), s32[128,1,8]{2,1,0:T(1,128)S(1)}, u32[]{:S(2)}, u32[]{:S(2)}) %all-to-all-start) | async-done | bytes 4128 | tf_op jit(solution)/shard_map/all_to_all | solution.py:51
  39.3 4.3 %stack.2 = bf16[128,32,1024]{2,1,0:T(8,128)(2,1)} broadcast(bf16[32,1024]{1,0:T(8,128)(2,1)S(1)} %copy-done.4), dimensions={1,2} | broadcast | bytes 8454144 | tf_op jit(solution)/shard_map/stack | solution.py:12
  43.5 5.8 %all-to-all-start.1 = ((bf16[128,32,1024]{2,1,0:T(8,128)(2,1)}), bf16[128,32,1024]{2,1,0:T(8,128)(2,1)}, u32[]{:S(2)}, u32[]{:S(2)}) async-start(bf16[128,32,1024]{2,1,0:T(8,128)(2,1)} %stack.2), calls=%async_computation.1 | async-start | bytes 16777216 | tf_op jit(solution)/shard_map/all_to_all | solution.py:11
  49.4 0.5 broadcast.394
  49.9 1.0 fusion.44
  51.0 6.7 %gather_fusion.1 = bf16[1024,512]{1,0:T(8,128)(2,1)S(1)} fusion(bf16[4096,512]{1,0:T(8,128)(2,1)} %param.13, s32[1024]{0:T(1024)S(1)} %broadcast_clamp_fusion.1), kind=kCustom, calls=%fused_computation.1 | custom fusion | bytes 2101248 | tf_op jit(solution)/shard_map/gather | solution.py:57
  57.8 1.3 copy.18
  59.2 7.5 %gather_fusion.2 = f32[1024,512]{1,0:T(8,128)} fusion(f32[2048,512]{1,0:T(8,128)} %param.9, s32[1024]{0:T(1024)S(1)} %broadcast_clamp_fusion), kind=kCustom, calls=%fused_computation.2 | custom fusion | bytes 4198400 | tf_op jit(solution)/shard_map/gather | solution.py:56
  66.7 6.9 %scatter_custom_fusion.2 = s32[2049]{0:T(1024)S(1)} fusion(s32[1024]{0:T(1024)S(1)} %bitcast.54, s32[1024]{0:T(1024)S(1)} %reshape.294, s32[]{:T(128)} %constant.21.clone.1), kind=kCustom, calls=%fused_computation.66 | custom fusion | flops 1024 | bytes 8200 | tf_op jit(solution)/shard_map/scatter-add | solution.py:62
  73.7 1.8 fusion.66
  75.5 0.2 copy-done.3
  75.7 1.8 fusion.61
  77.5 2.9 %fusion.64 = (bf16[1024,512]{1,0:T(8,128)(2,1)S(1)}, f32[1024,512]{1,0:T(8,128)}) fusion(f32[1024,512]{1,0:T(8,128)S(1)} %copy-done.2, f32[1024,1536]{1,0:T(8,128)S(1)} %fusion.61, f32[1024,1536]{1,0:T(8,128)S(1)} %fusion.66), kind=kLoop, calls=%fused_computation.106 | loop fusion | flops 8912896 | bytes 17825792 | tf_op jit(solution)/shard_map/convert_element_type | solution.py:66
  80.3 10.2 %scatter_custom_fusion.1 = f32[2049,512]{1,0:T(8,128)} fusion(s32[1024]{0:T(1024)S(1)} %bitcast.55, f32[]{:T(128)} %constant.19.clone.1, f32[1024,512]{1,0:T(8,128)} %get-tuple-element.5, f32[1024,512]{1,0:T(8,128)} %gather_fusion.2), kind=kCustom, calls=%fused_computation.21 | custom fusion | flops 2097152 | bytes 8390660 | tf_op jit(solution)/shard_map/scatter-add | solution.py:61
  90.5 94.2 %all-gather.3.cloned.1.call-done = bf16[128,4,4096]{2,1,0:T(4,128)(2,1)} async-done(((bf16[1,4,4096]{2,1,0:T(4,128)(2,1)}), bf16[128,4,4096]{2,1,0:T(4,128)(2,1)}) %all-gather.3.cloned.1.call-update) | async-done | bytes 4194320 | tf_op jit(solution)/shard_map/all_gather | solution.py:77
  184.7 6.9 %reshape.300 = bf16[512,4096]{1,0:T(8,128)(2,1)} reshape(bf16[128,4,4096]{2,1,0:T(4,128)(2,1)} %all-gather.3.cloned.1.call-done) | data formatting | bytes 8388608
  191.6 18.2 %multiply_reduce_fusion = f32[1024]{0:T(1024)S(1)} fusion(bf16[1024,512]{0,1:T(8,128)(2,1)} %copy.18, bf16[512,4096]{1,0:T(8,128)(2,1)} %reshape.300, bf16[4096,1024]{1,0:T(8,128)(2,1)} %bitcast.11, bf16[1024,512]{1,0:T(8,128)(2,1)S(1)} %gather_fusion.1, bf16[1024,512]{1,0:T(8,128)(2,1)S(1)} %get-tuple-element.4), kind=kOutput, calls=%fused_computation.42 | convolution fusion | flops 12928416768 | bytes 15732736 | tf_op jit(solution)/shard_map/dot_general | solution.py:75
  209.8 0.7 div.84
  210.5 5.3 %all-to-all-start.2 = ((f32[128,1,8]{2,1,0:T(1,128)}), f32[128,1,8]{2,1,0:T(1,128)S(1)}, u32[]{:S(2)}, u32[]{:S(2)}) async-start(f32[128,1,8]{2,1,0:T(1,128)} %bitcast.13), calls=%async_computation.2 | async-start | bytes 131072 | tf_op jit(solution)/shard_map/all_to_all | solution.py:82
  215.9 6.1 %fusion.10 = f32[2048,512]{1,0:T(8,128)} fusion(f32[2048,512]{1,0:T(8,128)} %param.9, f32[2049,512]{1,0:T(8,128)} %scatter_custom_fusion.1, f32[2048]{0:T(1024)S(1)} %fusion.45), kind=kLoop, calls=%fused_computation.18 | loop fusion | flops 2097152 | bytes 12591104 | tf_op jit(solution)/shard_map/add | solution.py:65
  222.0 3.3 %all-to-all-done.2 = f32[128,1,8]{2,1,0:T(1,128)S(1)} async-done(((f32[128,1,8]{2,1,0:T(1,128)}), f32[128,1,8]{2,1,0:T(1,128)S(1)}, u32[]{:S(2)}, u32[]{:S(2)}) %all-to-all-start.2) | async-done | bytes 4128 | tf_op jit(solution)/shard_map/all_to_all | solution.py:82
  225.3 0.5 broadcast.395
  225.8 0.8 reduce.11
  226.7 3.4 %gather_fusion.3 = f32[512]{0:T(512)} fusion(f32[1024]{0:T(1024)S(1)} %reshape.240, s32[1024]{0:T(1024)S(1)} %pad_clamp_fusion), kind=kCustom, calls=%fused_computation.3 | custom fusion | bytes 6144 | tf_op jit(solution)/shard_map/gather | solution.py:85
  (34 shorter events, 0.7 us)
Async XLA Ops:
  7.2 66.5 %copy-start = (bf16[512,1536]{1,0:T(8,128)(2,1)S(1)}, bf16[512,1536]{1,0:T(8,128)(2,1)}, u32[]{:S(2)}) copy-start(bf16[512,1536]{1,0:T(8,128)(2,1)} %param.14) | copy-start | bytes 4718596
  7.2 7.8 %copy-start.5 = (s32[512]{0:T(512)S(1)}, s32[512]{0:T(512)}, u32[]{:S(2)}) copy-start(s32[512]{0:T(512)} %param.12) | copy-start | bytes 6148
  7.2 32.1 %copy-start.4 = (bf16[32,1024]{1,0:T(8,128)(2,1)S(1)}, bf16[32,1024]{1,0:T(8,128)(2,1)}, u32[]{:S(2)}) copy-start(bf16[32,1024]{1,0:T(8,128)(2,1)} %param.16) | copy-start | bytes 196612
  18.4 20.8 %all-to-all-start = ((s32[128,1,8]{2,1,0:T(1,128)}), s32[128,1,8]{2,1,0:T(1,128)S(1)}, u32[]{:S(2)}, u32[]{:S(2)}) async-start(s32[128,1,8]{2,1,0:T(1,128)} %bitcast.7), calls=%async_computation | async-start | bytes 131072 | tf_op jit(solution)/shard_map/all_to_all | solution.py:51
  29.9 154.8 %all-gather.3.cloned.1.call-start = ((), (), s32[]{:S(2)}) async-start(), calls=%async_computation.3 | async-start | bytes 4227072 | tf_op jit(solution)/shard_map/all_gather | solution.py:77
  43.5 148.1 %all-to-all-start.1 = ((bf16[128,32,1024]{2,1,0:T(8,128)(2,1)}), bf16[128,32,1024]{2,1,0:T(8,128)(2,1)}, u32[]{:S(2)}, u32[]{:S(2)}) async-start(bf16[128,32,1024]{2,1,0:T(8,128)(2,1)} %stack.2), calls=%async_computation.1 | async-start | bytes 16777216 | tf_op jit(solution)/shard_map/all_to_all | solution.py:11
  73.6 1.8 copy-start.2
  73.7 2.0 copy-start.3
  210.5 14.7 %all-to-all-start.2 = ((f32[128,1,8]{2,1,0:T(1,128)}), f32[128,1,8]{2,1,0:T(1,128)S(1)}, u32[]{:S(2)}, u32[]{:S(2)}) async-start(f32[128,1,8]{2,1,0:T(1,128)} %bitcast.13), calls=%async_computation.2 | async-start | bytes 131072 | tf_op jit(solution)/shard_map/all_to_all | solution.py:82
  215.9 14.2 %copy-start.1 = (bf16[512,1536]{1,0:T(8,128)(2,1)S(1)}, bf16[512,1536]{1,0:T(8,128)(2,1)}, u32[]{:S(2)}) copy-start(bf16[512,1536]{1,0:T(8,128)(2,1)} %param.14) | copy-start | bytes 4718596
Sparse Core Ops, SparseCore 0:
  33.9 150.7 all-gather.2
